TPU v7x, 768 devices: a whole 4x8x12 slice. The times are simulated.
768 devices in a mesh: dp: 4 (over x), pipe: 12 (over z), ctx: 16 (over y, core).
Axes of the slice: x: 4, y: 8, z: 12, core: 2. Of those that a mesh axis runs over, the one named last changes fastest.
Arguments:
- ssm_input: bfloat16 [4, 12, 4096, 1024], P('dp', 'pipe', 'ctx'), may hold values from -6 to 6
- state_write: bfloat16 [4, 12, 4096, 128], P('dp', 'pipe', 'ctx'), may hold values from -0.1875 to 0.1875
- state_read: bfloat16 [4, 12, 4096, 128], P('dp', 'pipe', 'ctx'), may hold values from -0.1875 to 0.1875
- step_raw: bfloat16 [4, 12, 4096, 16], P('dp', 'pipe', 'ctx'), may hold values from -6 to 6
- decay_log: float32 [12, 16], P('pipe'), may hold values from -20 to -3
- step_bias: float32 [12, 16], P('pipe'), may hold values from -1 to 1
- skip_gain: float32 [12, 16], P('pipe'), may hold values from 0.5 to 1.5
- out_grad: bfloat16 [4, 12, 4096, 1024], P('dp', 'pipe', 'ctx'), may hold values from -6 to 6
Outputs:
- ssm_output: bfloat16 [4, 12, 4096, 1024], P('dp', 'pipe', 'ctx')
- prev_grad_x: bfloat16 [4, 12, 4096, 1024], P('dp', 'pipe', 'ctx')
- prev_grad_write: bfloat16 [4, 12, 4096, 128], P('dp', 'pipe', 'ctx')
- prev_grad_read: bfloat16 [4, 12, 4096, 128], P('dp', 'pipe', 'ctx')
- prev_grad_step: bfloat16 [4, 12, 4096, 16], P('dp', 'pipe', 'ctx')
- param_grads: float32 [12, 3, 16], P('pipe')
All inputs are finite; a program needn't handle non-finite values.
Results may differ from a plain program's by a relative error of at most 0.008.
Values may be sent and summed in bfloat16 or wider, within the bound.
No kernel may reach another device: no remote copies, remote signals or barrier semaphores. Data moves between devices by JAX's collectives and lax.ppermute only.
A program may use at most 64 MiB of HBM per device.

v0:
```python
import jax
import jax.numpy as jnp
from jax import lax
from jax.experimental import pallas as pl
from jax.experimental.pallas import tpu as pltpu
from jax.sharding import Mesh
from jax.sharding import PartitionSpec as P

HEADS = 16
HEAD_DIM = 64
STATE = 128
BLOCK = 256
WIDTH = HEADS * HEAD_DIM
RANKS = 16
CTX = ("ctx_0", "ctx_1")
DP_CTX = ("dp", "ctx_0", "ctx_1")
F32 = jnp.float32
BF16 = jnp.bfloat16
LOG2E = 1.4426950408889634
CLAMP = 64.0
INTERPRET = False


def mm(a, b, dims, precision=None):
    return lax.dot_general(
        a, b, (dims, ((), ())), precision=precision, preferred_element_type=F32
    )


def exact(a, b, dims):
    return mm(a, b, dims, lax.Precision.HIGHEST)


def parts_mm(ones, value, dims):
    total = None
    for piece in split(value, 3):
        term = mm(ones, piece, dims)
        total = term if total is None else total + term
    return total


def triangle(lower):
    row = lax.broadcasted_iota(jnp.int32, (BLOCK, BLOCK), 0)
    col = lax.broadcasted_iota(jnp.int32, (BLOCK, BLOCK), 1)
    return row >= col if lower else row <= col


def head_of_lane():
    head = lax.broadcasted_iota(jnp.int32, (HEADS, WIDTH), 0)
    lane = lax.broadcasted_iota(jnp.int32, (HEADS, WIDTH), 1)
    return jnp.where((lane >= head * HEAD_DIM) & (lane < (head + 1) * HEAD_DIM), 1.0, 0.0)


def split(value, parts):
    pieces = []
    for _ in range(parts):
        piece = value.astype(BF16)
        pieces.append(piece)
        value = value - piece.astype(F32)
    return pieces


def expand(value, spread, parts=2):
    pieces = jnp.concatenate(split(value, parts), axis=1)
    return mm(pieces, jnp.concatenate([spread] * parts, axis=0), ((1,), (0,)))


def per_head(value, spread, parts=2):
    total = None
    for piece in split(value, parts):
        term = mm(piece, spread, ((1,), (1,)))
        total = term if total is None else total + term
    return total


ANY = pl.BlockSpec(memory_space=pltpu.HBM)
VMEM = pl.BlockSpec(memory_space=pltpu.VMEM)


def shape(dims, dtype):
    return jax.ShapeDtypeStruct(dims, dtype)


def chunks_of(dims):
    return 4 if dims[0] * dims[1] >= BLOCK * WIDTH else 1


def run_kernel(body, fetched, held, outs, scratch=()):
    count, near, far = len(fetched), len(held), len(outs)
    sem_count = max(count, 1)

    def kernel(*refs):
        sources = refs[:count]
        blocks = refs[count + near + far : 2 * count + near + far]
        sems = refs[2 * count + near + far]
        rest = refs[2 * count + near + far + 1 :]
        copies = []
        for k, (src, dst) in enumerate(zip(sources, blocks)):
            count_of = chunks_of(src.shape)
            rows = src.shape[0] // count_of
            copies.append(
                [
                    pltpu.make_async_copy(
                        src.at[pl.ds(i * rows, rows)], dst.at[pl.ds(i * rows, rows)], sems.at[k, i]
                    )
                    for i in range(count_of)
                ]
            )
        for group in copies:
            for copy in group:
                copy.start()

        def fetch(k):
            for copy in copies[k]:
                copy.wait()
            return blocks[k]

        body(fetch, *refs[count : count + near + far], *rest)

    return pl.pallas_call(
        kernel,
        out_shape=outs,
        in_specs=[ANY] * count + [VMEM] * near,
        out_specs=tuple([VMEM] * far),
        scratch_shapes=[pltpu.VMEM(v.shape, v.dtype) for v in fetched]
        + [pltpu.SemaphoreType.DMA((sem_count, 4))]
        + list(scratch),
        interpret=INTERPRET,
        compiler_params=pltpu.CompilerParams(vmem_limit_bytes=24 * 1024 * 1024),
    )(*(pltpu.with_memory_space_constraint(v, pltpu.HBM) for v in fetched), *held)


def identity(size):
    row = lax.broadcasted_iota(jnp.int32, (size, size), 0)
    col = lax.broadcasted_iota(jnp.int32, (size, size), 1)
    return jnp.where(row == col, 1.0, 0.0)


def upright(raw_ref):
    return mm(identity(BLOCK).astype(BF16), raw_ref[...], ((1,), (1,)))


def ends_kernel(fetch, pay_ref, time_ref):
    spread = head_of_lane().astype(BF16)
    raw = upright(fetch(0)) + fetch(2)[...]
    step = jnp.maximum(raw, 0.0) + jnp.log1p(jnp.exp(-jnp.abs(raw)))
    rate = step * -jnp.exp(fetch(1)[...])
    run = parts_mm(jnp.where(triangle(True), 1.0, 0.0).astype(BF16), rate, ((1,), (0,)))
    last = run[BLOCK - 1 : BLOCK, :]
    time_ref[0:BLOCK, :] = step
    time_ref[BLOCK : 2 * BLOCK, :] = run
    drop = jnp.exp(last)
    upper_half = lax.broadcasted_iota(jnp.int32, (8, STATE), 0) < 4
    for h in range(HEADS):
        high = jnp.broadcast_to(drop[:, h : h + 1], (8, STATE))
        piece = high.astype(BF16).astype(F32)
        pay_ref[h, 128:136, :] = jnp.where(upper_half, piece, high - piece).astype(BF16)
    head = expand(jnp.exp(run), spread)
    tail = expand(jnp.exp(last - run) * step, spread)
    gs = (fetch(3)[...].astype(F32) * head).astype(BF16)
    seen = mm(fetch(4)[...], gs, ((0,), (0,))).T.astype(BF16)
    for h in range(HEADS):
        pay_ref[h, 64:128, :] = seen[h * HEAD_DIM : (h + 1) * HEAD_DIM, :]
    xs = (fetch(5)[...].astype(F32) * tail).astype(BF16)
    end = mm(fetch(6)[...], xs, ((0,), (0,))).T.astype(BF16)
    for h in range(HEADS):
        pay_ref[h, 0:64, :] = end[h * HEAD_DIM : (h + 1) * HEAD_DIM, :]


PACK = WIDTH + 2 * STATE
SENT = WIDTH // HEAD_DIM + 9


def column(k):
    return slice(2 * STATE + k * HEADS, 2 * STATE + (k + 1) * HEADS)


def inner_kernel(
    fetch, time_ref, lead_ref, pack_ref, out_ref, y_ref, blank_ref, dx_ref, acc_ref
):
    blank_ref[...] = jnp.zeros(blank_ref.shape, F32)
    causal = triangle(True)
    step = time_ref[0:BLOCK, :]
    run = time_ref[BLOCK : 2 * BLOCK, :]
    last = run[BLOCK - 1 : BLOCK, :]
    running = run * LOG2E
    across = exact(jnp.log(step) * LOG2E - running, identity(BLOCK), ((0,), (0,)))
    lane = lax.broadcasted_iota(jnp.int32, (1, 2 * HEAD_DIM), 1)
    halves = [
        jnp.where(lane < HEAD_DIM, 1.0, 0.0).astype(BF16),
        jnp.where(lane >= HEAD_DIM, 1.0, 0.0).astype(BF16),
    ]
    b = fetch(2)[...]
    c = fetch(3)[...]
    scores = jnp.where(causal, mm(c, b, ((1,), (1,))), 0.0)
    x_ref = fetch(0)
    g_ref = fetch(1)
    for pair in range(HEADS // 2):
        lanes = slice(pair * 128, (pair + 1) * 128)
        xp = x_ref[:, lanes]
        gp = g_ref[:, lanes]
        y = None
        dx = None
        for i in range(2):
            h = 2 * pair + i
            xm = xp * halves[i]
            gm = gp * halves[i]
            spread = jnp.minimum(running[:, h : h + 1] + across[h : h + 1, :], CLAMP)
            decay = jnp.exp2(spread)
            weight = (scores * decay).astype(BF16)
            y_part = mm(weight, xm, ((1,), (0,)))
            dx_part = mm(weight, gm, ((0,), (0,)))
            y = y_part if y is None else y + y_part
            dx = dx_part if dx is None else dx + dx_part
            grad = mm(gp, xm, ((1,), (1,))).astype(BF16).astype(F32) * decay
            if h == 0:
                acc_ref[...] = grad
            else:
                acc_ref[...] += grad
        dx_ref[:, lanes] = dx
        y_ref[:, lanes] = y
    grad = jnp.where(causal, acc_ref[...], 0.0).astype(BF16)
    out_ref[:, 0:STATE] = mm(grad, c, ((0,), (0,)))
    out_ref[:, STATE : 2 * STATE] = mm(grad, b, ((1,), (0,)))
    spread = head_of_lane().astype(BF16)
    x = x_ref[...].astype(F32)
    g = g_ref[...].astype(F32)
    dx = dx_ref[...]
    y = y_ref[...]
    gain = expand(jnp.broadcast_to(fetch(7)[...], (8, HEADS)), spread, 3)[0:1, :]
    reads = per_head(g * y, spread)
    writes = per_head(x * dx, spread)
    y_ref[...] = y + gain * x
    head = jnp.exp(run)
    tail = jnp.exp(last - run) * step
    high, low = split(tail, 2)
    lead_ref[:, 0:WIDTH] = (dx + gain * g).astype(BF16)
    lead_ref[:, WIDTH : WIDTH + STATE] = b
    lead_ref[:, WIDTH + STATE : WIDTH + STATE + 2 * HEADS] = jnp.concatenate([high, low], axis=1)
    pack_ref[:, 0:WIDTH] = (x * expand(tail, spread)).astype(BF16)
    pack_ref[:, WIDTH : 2 * WIDTH] = (g * expand(head, spread)).astype(BF16)
    pack_ref[:, 2 * WIDTH : 2 * WIDTH + STATE] = b
    pack_ref[:, 2 * WIDTH + STATE : 2 * WIDTH + 2 * STATE] = c
    skips = jnp.broadcast_to(jnp.sum(g * x, axis=0, keepdims=True), (8, WIDTH))
    skips = per_head(skips, spread, 3)[0:1, :]
    raw = upright(fetch(4)) + fetch(6)[...]
    slope = -jnp.exp(fetch(5)[...])
    out_ref[:, column(0)] = reads
    out_ref[:, column(1)] = writes
    out_ref[:, column(2)] = step
    out_ref[:, column(3)] = 1.0 / (1.0 + jnp.exp(-raw))
    out_ref[:, column(4)] = jnp.broadcast_to(slope, (BLOCK, HEADS))
    out_ref[:, column(5)] = jnp.broadcast_to(jnp.exp(last), (BLOCK, HEADS))
    out_ref[:, column(6)] = head
    out_ref[:, column(7)] = jnp.broadcast_to(skips, (BLOCK, HEADS))


def join_kernel(fetch, got_ref, acc_ref, out_ref):
    def drop_of(j):
        return got_ref[j, 128:129, :].astype(F32) + got_ref[j, 132:133, :].astype(F32)

    state = jnp.zeros((64, STATE), F32)
    later = jnp.zeros((64, STATE), F32)
    for j in range(RANKS):
        k = RANKS - 1 - j
        out_ref[j, 0:64, :] = state.astype(BF16)
        out_ref[k, 64:128, :] = later.astype(BF16)
        state = state * drop_of(j) + got_ref[j, 0:64, :].astype(F32)
        later = later * drop_of(k) + got_ref[k, 64:128, :].astype(F32)


def outer_kernel(blank_ref, state_ref, pack_ref, acc_ref, par_out, sent_out, par_ref, sent_ref, sems):
    copies = [
        pltpu.make_async_copy(state_ref.at[:, 64:128, :], sent_out.at[0:HEADS], sems.at[0]),
        pltpu.make_async_copy(par_ref, par_out, sems.at[1]),
        pltpu.make_async_copy(sent_ref, sent_out.at[HEADS:SENT], sems.at[2]),
    ]
    copies[0].start()
    spread = head_of_lane().astype(BF16)
    start = state_ref[:, 0:64, :].reshape(WIDTH, STATE)
    later = state_ref[:, 64:128, :].reshape(WIDTH, STATE)
    both = (start.astype(F32) * later.astype(F32)).astype(BF16)
    carried = mm(jnp.ones((8, STATE), BF16), both, ((1,), (1,)))
    carried = per_head(carried, spread)[0:1, :]
    xs = pack_ref[:, 0:WIDTH]
    gs = pack_ref[:, WIDTH : 2 * WIDTH]
    back = mm(pack_ref[:, 2 * WIDTH : 2 * WIDTH + STATE], later, ((1,), (1,)))
    tails = per_head(back * xs.astype(F32), spread, 1)
    front = mm(pack_ref[:, 2 * WIDTH + STATE : 2 * WIDTH + 2 * STATE], start, ((1,), (1,)))
    reads = acc_ref[:, column(0)] + per_head(front * gs.astype(F32), spread, 1)
    writes = acc_ref[:, column(1)] + tails
    step = acc_ref[:, column(2)]
    slope = acc_ref[0:1, column(4)]
    ends = jnp.sum(tails, axis=0, keepdims=True) + acc_ref[0:1, column(5)] * carried
    upper = jnp.where(triangle(False), 1.0, 0.0).astype(BF16)
    d_rate = parts_mm(upper, reads - writes, ((1,), (0,))) + ends
    d_raw = (d_rate * slope + writes / step) * acc_ref[:, column(3)]
    rates = jnp.sum(d_rate * step, axis=0, keepdims=True) * slope
    biases = jnp.sum(d_raw, axis=0, keepdims=True)
    flat = jnp.concatenate([rates, biases, acc_ref[0:1, column(7)]], axis=1)
    for k in range(par_ref.shape[0]):
        par_ref[k, :, 0 : 3 * HEADS] = flat
    copies[1].start()
    draw = mm(d_raw.astype(BF16), identity(BLOCK).astype(BF16), ((0,), (0,))).astype(BF16)
    sent_ref[8, 0:HEADS, :] = draw[:, 0:128]
    sent_ref[8, HEADS : 2 * HEADS, :] = draw[:, 128:256]
    db = acc_ref[:, 0:STATE] + mm(xs, later, ((1,), (0,)))
    sent_ref[0:4, :, :] = db.astype(BF16).reshape(4, HEAD_DIM, STATE)
    dc = acc_ref[:, STATE : 2 * STATE] + mm(gs, start, ((1,), (0,)))
    sent_ref[4:8, :, :] = dc.astype(BF16).reshape(4, HEAD_DIM, STATE)
    copies[2].start()
    for copy in copies:
        copy.wait()


def output_kernel(fetch, state_ref, pack_ref, acc_ref, base_ref, y_ref):
    spread = head_of_lane().astype(BF16)
    start = state_ref[:, 0:64, :].reshape(WIDTH, STATE)
    front = mm(pack_ref[:, 2 * WIDTH + STATE : 2 * WIDTH + 2 * STATE], start, ((1,), (1,)))
    head = expand(acc_ref[:, column(6)], spread)
    y_ref[...] = (base_ref[...] + front * head).astype(BF16).reshape(y_ref.shape)


def received_kernel(
    lead_ref, sent_ref, dx_out, db_out, dc_out, draw_out, dx_ref, sems
):
    copies = [
        pltpu.make_async_copy(
            sent_ref.at[HEADS + 4 * k + i],
            out.at[0, 0, pl.ds(i * HEAD_DIM, HEAD_DIM)],
            sems.at[4 * k + i],
        )
        for k, out in enumerate((db_out, dc_out))
        for i in range(4)
    ]
    copies += [
        pltpu.make_async_copy(
            sent_ref.at[HEADS + 8, pl.ds(i * HEADS, HEADS)],
            draw_out.at[0, 0, :, pl.ds(i * 128, 128)],
            sems.at[8 + i],
        )
        for i in range(2)
    ]
    for copy in copies:
        copy.start()
    spread = head_of_lane().astype(BF16)
    spread = jnp.concatenate([spread, spread], axis=0)
    at = WIDTH + STATE
    b = lead_ref[:, WIDTH:at]
    factors = lead_ref[:, at : at + 2 * HEADS]
    for k in range(4):
        lanes = slice(k * 256, (k + 1) * 256)
        later = sent_ref[4 * k : 4 * k + 4, :, :].reshape(256, STATE)
        back = mm(b, later, ((1,), (1,))) * mm(factors, spread[:, lanes], ((1,), (0,)))
        dx_ref[:, lanes] = (lead_ref[:, lanes].astype(F32) + back).astype(BF16)
        copy = pltpu.make_async_copy(
            dx_ref.at[:, pl.ds(k * 256, 256)],
            dx_out.at[0, 0, :, pl.ds(k * 256, 256)],
            sems.at[10 + k],
        )
        copy.start()
        copies.append(copy)
    for copy in copies:
        copy.wait()


def fold_kernel(fetch, got_ref, out_ref):
    flat = jnp.sum(got_ref[...], axis=0)
    for k in range(3):
        out_ref[k, :, :] = flat[:, k * HEADS : (k + 1) * HEADS]


def spread_out(value, axes):
    return lax.all_to_all(value, axes, 0, 0, tiled=True)


def relay(value):
    size = lax.axis_size("pipe")
    return lax.ppermute(value, "pipe", [(i, i - 1) for i in range(1, size)])


def layer(x, b, c, raw, log_row, bias_row, gain_row, g):
    x, b, c, raw, g = (v[0, 0] for v in (x, b, c, raw, g))
    raw = raw.T
    everyone = 1
    for name in DP_CTX:
        everyone *= lax.axis_size(name)
    pay, time = run_kernel(
        ends_kernel,
        (raw, log_row, bias_row, g, c, x, b),
        (),
        (shape((HEADS, 136, STATE), BF16), shape((2 * BLOCK, HEADS), F32)),
    )
    got = spread_out(pay, CTX)
    lead, pack, acc, base, blank = run_kernel(
        inner_kernel,
        (x, g, b, c, raw, log_row, bias_row, gain_row),
        (time,),
        (
            shape((BLOCK, PACK), BF16),
            shape((BLOCK, 2 * WIDTH + 2 * STATE), BF16),
            shape((BLOCK, 2 * STATE + 8 * HEADS), F32),
            shape((BLOCK, WIDTH), F32),
            shape((everyone, 1, 128), F32),
        ),
        (pltpu.VMEM((BLOCK, WIDTH), F32), pltpu.VMEM((BLOCK, BLOCK), F32)),
    )
    lead = relay(lead)
    (states,) = run_kernel(join_kernel, (), (got, acc), (shape((RANKS, 128, STATE), BF16),))
    states = spread_out(states, CTX)
    blank = pltpu.with_memory_space_constraint(blank, pltpu.HBM)
    par, sent = pl.pallas_call(
        outer_kernel,
        out_shape=(shape((everyone, 1, 128), F32), shape((SENT, HEAD_DIM, STATE), BF16)),
        in_specs=[ANY] + [VMEM] * 3,
        out_specs=(ANY, ANY),
        input_output_aliases={0: 0},
        scratch_shapes=[
            pltpu.VMEM((everyone, 1, 128), F32),
            pltpu.VMEM((9, HEAD_DIM, STATE), BF16),
            pltpu.SemaphoreType.DMA((3,)),
        ],
        interpret=INTERPRET,
        compiler_params=pltpu.CompilerParams(vmem_limit_bytes=24 * 1024 * 1024),
    )(blank, states, pack, acc)
    sent = relay(sent)
    par = spread_out(par, DP_CTX)
    (y,) = run_kernel(
        output_kernel, (), (states, pack, acc, base), (shape((1, 1, BLOCK, WIDTH), BF16),)
    )
    dx, db, dc, draw = pl.pallas_call(
        received_kernel,
        out_shape=(
            shape((1, 1, BLOCK, WIDTH), BF16),
            shape((1, 1, BLOCK, STATE), BF16),
            shape((1, 1, BLOCK, STATE), BF16),
            shape((1, 1, HEADS, BLOCK), BF16),
        ),
        in_specs=[VMEM] * 2,
        out_specs=(ANY, ANY, ANY, ANY),
        scratch_shapes=[pltpu.VMEM((BLOCK, WIDTH), BF16), pltpu.SemaphoreType.DMA((14,))],
        interpret=INTERPRET,
        compiler_params=pltpu.CompilerParams(vmem_limit_bytes=12 * 1024 * 1024),
    )(lead, sent)
    (par,) = run_kernel(fold_kernel, (), (par,), (shape((3, 1, HEADS), F32),))
    return y, dx, db, dc, jnp.swapaxes(draw, 2, 3), jnp.swapaxes(par, 0, 1)


def solution(mesh):
    finer = Mesh(
        mesh.devices.reshape(mesh.shape["dp"], mesh.shape["pipe"], mesh.shape["ctx"] // 2, 2),
        ("dp", "pipe", "ctx_0", "ctx_1"),
    )
    tokens = P("dp", "pipe", CTX, None)
    row = P("pipe", None)
    return jax.shard_map(
        layer,
        mesh=finer,
        in_specs=(tokens, tokens, tokens, tokens, row, row, row, tokens),
        out_specs=(tokens, tokens, tokens, tokens, tokens, P("pipe", None, None)),
        check_vma=False,
    )
```

profile of v0, /device:TPU:1, one launch (start us, length us, event | category | flops | bytes accessed | tf_op | source)
XLA Modules:
  0.0 77.9 jit_solution(17863163416882215447)
XLA Ops:
  0.6 3.7 %shard_map.127 = (bf16[16,136,128]{2,1,0:T(8,128)(2,1)}, f32[512,16]{1,0:T(8,128)S(1)}) custom-call(bf16[16,256]{1,0:T(8,128)(2,1)} %bitcast.17, f32[1,16]{1,0:T(1,128)} %refs_5_.1, f32[1,16]{1,0:T(1,128)} %refs_6_.1, bf16[256,1024]{1,0:T(8,128)(2,1)} %bitcast.9, bf16[256,128]{1,0:T(8,128)(2,1)} %bitcast.13, bf16[256,1024]{1,0:T(8,128)(2,1)} %bitcast.11, ...), custom_call_target="tpu_custom_call" | custom-call | tf_op jit(solution)/shard_map/pallas_call | solution.py:120
  4.3 13.9 %all-to-all-start = ((bf16[16,136,128]{2,1,0:T(8,128)(2,1)}), bf16[16,136,128]{2,1,0:T(8,128)(2,1)S(1)}, u32[]{:S(2)}, u32[]{:S(2)}) async-start(bf16[16,136,128]{2,1,0:T(8,128)(2,1)} %get-tuple-element.19), calls=%async_computation | async-start | bytes 1114112 | tf_op jit(solution)/shard_map/all_to_all | solution.py:374
  18.2 6.3 %shard_map.128 = (bf16[256,1280]{1,0:T(8,128)(2,1)S(1)}, bf16[256,2304]{1,0:T(8,128)(2,1)S(1)}, f32[256,384]{1,0:T(8,128)S(1)}, f32[256,1024]{1,0:T(8,128)S(1)}, f32[64,1,128]{2,1,0:T(1,128)S(1)}) custom-call(bf16[256,1024]{1,0:T(8,128)(2,1)} %bitcast.12, bf16[256,1024]{1,0:T(8,128)(2,1)} %bitcast.10, bf16[256,128]{1,0:T(8,128)(2,1)} %bitcast.16, ...), custom_call_target="tpu_custom_call" | custom-call | tf_op jit(solution)/shard_map/pallas_call | solution.py:120
  24.5 0.0 copy-start
  24.5 1.0 %copy-done = f32[256,1024]{1,0:T(8,128)} copy-done((f32[256,1024]{1,0:T(8,128)}, f32[256,1024]{1,0:T(8,128)S(1)}, u32[]{:S(2)}) %copy-start) | copy-done | bytes 1048600
  25.5 0.0 copy-start.2
  25.5 0.6 copy-done.2
  26.1 0.9 %copy-done.3 = bf16[256,1280]{1,0:T(8,128)(2,1)} copy-done((bf16[256,1280]{1,0:T(8,128)(2,1)}, bf16[256,1280]{1,0:T(8,128)(2,1)S(1)}, u32[]{:S(2)}) %copy-start.3) | copy-done | bytes 655384
  26.9 9.2 %all-to-all-done.refs_0_ = bf16[16,136,128]{2,1,0:T(8,128)(2,1)S(1)} async-done(((bf16[16,136,128]{2,1,0:T(8,128)(2,1)}), bf16[16,136,128]{2,1,0:T(8,128)(2,1)S(1)}, u32[]{:S(2)}, u32[]{:S(2)}) %all-to-all-start) | async-done | bytes 557088 | tf_op jit(solution)/shard_map/all_to_all | solution.py:374
  36.2 1.0 %shard_map.129 = bf16[16,128,128]{2,1,0:T(8,128)(2,1)} custom-call(bf16[16,136,128]{2,1,0:T(8,128)(2,1)S(1)} %all-to-all-done.refs_0_, f32[256,384]{1,0:T(8,128)S(1)} %get-tuple-element.21.refs_1_.refs_2_.acc_ref), custom_call_target="tpu_custom_call" | custom-call | tf_op jit(solution)/shard_map/pallas_call | solution.py:120
  37.1 3.5 %all-to-all-start.1 = ((bf16[16,128,128]{2,1,0:T(8,128)(2,1)}), bf16[16,128,128]{2,1,0:T(8,128)(2,1)S(1)}, u32[]{:S(2)}, u32[]{:S(2)}) async-start(bf16[16,128,128]{2,1,0:T(8,128)(2,1)} %shard_map.129), calls=%async_computation.1 | async-start | bytes 1048576 | tf_op jit(solution)/shard_map/all_to_all | solution.py:374
  40.6 0.0 copy-start.1
  40.7 1.4 %collective-permute-start = (bf16[256,1280]{1,0:T(8,128)(2,1)}, bf16[256,1280]{1,0:T(8,128)(2,1)}, u32[]{:S(2)}, u32[]{:S(2)}) collective-permute-start(bf16[256,1280]{1,0:T(8,128)(2,1)} %copy-done.3), channel_id=1, source_target_pairs={{16,0},{32,16},{48,32},{64,48},{80,64},{96,80},{112,96},{128,112},... | collective-permute-start | bytes 1966088 | tf_op jit(solution)/shard_map/ppermute | solution.py:379
  42.1 15.2 %all-to-all-done.1.refs_0_.state_ref = bf16[16,128,128]{2,1,0:T(8,128)(2,1)S(1)} async-done(((bf16[16,128,128]{2,1,0:T(8,128)(2,1)}), bf16[16,128,128]{2,1,0:T(8,128)(2,1)S(1)}, u32[]{:S(2)}, u32[]{:S(2)}) %all-to-all-start.1) | async-done | bytes 524320 | tf_op jit(solution)/shard_map/all_to_all | solution.py:374
  57.3 2.3 %shard_map.131 = (f32[64,1,128]{2,1,0:T(1,128)}, bf16[25,64,128]{2,1,0:T(8,128)(2,1)}) custom-call(f32[64,1,128]{2,1,0:T(1,128)} %copy-done.2, bf16[16,128,128]{2,1,0:T(8,128)(2,1)S(1)} %all-to-all-done.1.refs_0_.state_ref, bf16[256,2304]{1,0:T(8,128)(2,1)S(1)} %get-tuple-element.22.refs_1_.pack_ref, ...), custom_call_target="tpu_custom_call", output_to_operand_aliasing={{0}: (0, {})} | custom-call | tf_op jit(solution)/shard_map/pallas_call | solution.py:412
  59.7 1.3 %collective-permute-start.1 = (bf16[25,64,128]{2,1,0:T(8,128)(2,1)}, bf16[25,64,128]{2,1,0:T(8,128)(2,1)S(1)}, u32[]{:S(2)}, u32[]{:S(2)}) collective-permute-start(bf16[25,64,128]{2,1,0:T(8,128)(2,1)} %get-tuple-element.26), channel_id=1, source_target_pairs={{16,0},{32,16},{48,32},{64,48},{80,64},{96,80},{112,96},{128,112},... | collective-permute-start | bytes 1228808 | tf_op jit(solution)/shard_map/ppermute | solution.py:379
  61.0 5.0 %all-to-all-start.2 = ((f32[64,1,128]{2,1,0:T(1,128)}), f32[64,1,128]{2,1,0:T(1,128)}, u32[]{:S(2)}, u32[]{:S(2)}) async-start(f32[64,1,128]{2,1,0:T(1,128)} %get-tuple-element.31), calls=%async_computation.2 | async-start | bytes 65536 | tf_op jit(solution)/shard_map/all_to_all | solution.py:374
  66.0 0.0 copy-done.1
  66.0 1.3 %shard_map.130 = bf16[1,1,256,1024]{3,2,1,0:T(8,128)(2,1)} custom-call(bf16[16,128,128]{2,1,0:T(8,128)(2,1)S(1)} %all-to-all-done.1.refs_0_.state_ref, bf16[256,2304]{1,0:T(8,128)(2,1)S(1)} %get-tuple-element.22.refs_1_.pack_ref, f32[256,384]{1,0:T(8,128)S(1)} %get-tuple-element.21.refs_1_.refs_2_.acc_ref, f32[256,1024]{1,0:T(8,128)S(1)} %copy-done.1), custom_call_target="tpu_custom_call" | custom-call | tf_op jit(solution)/shard_map/pallas_call | solution.py:120
  67.3 6.8 %all-to-all-done.2.refs_0_ = f32[64,1,128]{2,1,0:T(1,128)} async-done(((f32[64,1,128]{2,1,0:T(1,128)}), f32[64,1,128]{2,1,0:T(1,128)}, u32[]{:S(2)}, u32[]{:S(2)}) %all-to-all-start.2) | async-done | bytes 32800 | tf_op jit(solution)/shard_map/all_to_all | solution.py:374
  74.1 1.5 %shard_map.133 = f32[3,1,16]{2,1,0:T(1,128)} custom-call(f32[64,1,128]{2,1,0:T(1,128)} %all-to-all-done.2.refs_0_), custom_call_target="tpu_custom_call" | custom-call | tf_op jit(solution)/shard_map/pallas_call | solution.py:120
  75.6 0.0 collective-permute-done.lead_ref
  75.6 0.0 collective-permute-done.1.sent_ref
  75.6 2.3 %shard_map.132 = (bf16[1,1,256,1024]{3,2,1,0:T(8,128)(2,1)}, bf16[1,1,256,128]{3,2,1,0:T(8,128)(2,1)}, bf16[1,1,256,128]{3,2,1,0:T(8,128)(2,1)}, bf16[1,1,16,256]{3,2,1,0:T(8,128)(2,1)}) custom-call(bf16[256,1280]{1,0:T(8,128)(2,1)} %collective-permute-done.lead_ref, bf16[25,64,128]{2,1,0:T(8,128)(2,1)S(1)} %collective-permute-done.1.sent_ref), custom_call_target="tpu_custom_call" | custom-call | tf_op jit(solution)/shard_map/pallas_call | solution.py:431
  (1 shorter events, 0.0 us)
Async XLA Ops:
  4.3 31.8 %all-to-all-start = ((bf16[16,136,128]{2,1,0:T(8,128)(2,1)}), bf16[16,136,128]{2,1,0:T(8,128)(2,1)S(1)}, u32[]{:S(2)}, u32[]{:S(2)}) async-start(bf16[16,136,128]{2,1,0:T(8,128)(2,1)} %get-tuple-element.19), calls=%async_computation | async-start | bytes 1114112 | tf_op jit(solution)/shard_map/all_to_all | solution.py:374
  24.5 1.0 %copy-start = (f32[256,1024]{1,0:T(8,128)}, f32[256,1024]{1,0:T(8,128)S(1)}, u32[]{:S(2)}) copy-start(f32[256,1024]{1,0:T(8,128)S(1)} %get-tuple-element.23.refs_3_) | copy-start | bytes 3145732
  25.5 0.6 copy-start.2
  26.1 0.9 %copy-start.3 = (bf16[256,1280]{1,0:T(8,128)(2,1)}, bf16[256,1280]{1,0:T(8,128)(2,1)S(1)}, u32[]{:S(2)}) copy-start(bf16[256,1280]{1,0:T(8,128)(2,1)S(1)} %get-tuple-element.24) | copy-start | bytes 1966084
  37.1 20.1 %all-to-all-start.1 = ((bf16[16,128,128]{2,1,0:T(8,128)(2,1)}), bf16[16,128,128]{2,1,0:T(8,128)(2,1)S(1)}, u32[]{:S(2)}, u32[]{:S(2)}) async-start(bf16[16,128,128]{2,1,0:T(8,128)(2,1)} %shard_map.129), calls=%async_computation.1 | async-start | bytes 1048576 | tf_op jit(solution)/shard_map/all_to_all | solution.py:374
  40.6 25.3 %copy-start.1 = (f32[256,1024]{1,0:T(8,128)S(1)}, f32[256,1024]{1,0:T(8,128)}, u32[]{:S(2)}) copy-start(f32[256,1024]{1,0:T(8,128)} %copy-done) | copy-start | bytes 3145732
  40.7 34.9 %collective-permute-start = (bf16[256,1280]{1,0:T(8,128)(2,1)}, bf16[256,1280]{1,0:T(8,128)(2,1)}, u32[]{:S(2)}, u32[]{:S(2)}) collective-permute-start(bf16[256,1280]{1,0:T(8,128)(2,1)} %copy-done.3), channel_id=1, source_target_pairs={{16,0},{32,16},{48,32},{64,48},{80,64},{96,80},{112,96},{128,112},... | collective-permute-start | bytes 1966088 | tf_op jit(solution)/shard_map/ppermute | solution.py:379
  59.7 15.9 %collective-permute-start.1 = (bf16[25,64,128]{2,1,0:T(8,128)(2,1)}, bf16[25,64,128]{2,1,0:T(8,128)(2,1)S(1)}, u32[]{:S(2)}, u32[]{:S(2)}) collective-permute-start(bf16[25,64,128]{2,1,0:T(8,128)(2,1)} %get-tuple-element.26), channel_id=1, source_target_pairs={{16,0},{32,16},{48,32},{64,48},{80,64},{96,80},{112,96},{128,112},... | collective-permute-start | bytes 1228808 | tf_op jit(solution)/shard_map/ppermute | solution.py:379
  61.0 13.1 %all-to-all-start.2 = ((f32[64,1,128]{2,1,0:T(1,128)}), f32[64,1,128]{2,1,0:T(1,128)}, u32[]{:S(2)}, u32[]{:S(2)}) async-start(f32[64,1,128]{2,1,0:T(1,128)} %get-tuple-element.31), calls=%async_computation.2 | async-start | bytes 65536 | tf_op jit(solution)/shard_map/all_to_all | solution.py:374
where the time goes:
time: 78.4 us; the launch traced here: 77.9 us
  waiting for transfers between devices  31.3 us (40%)
  starting transfers between devices  25.1 us (32%)
  Pallas kernels  18.3 us (23%)
  local copies, waits for them, and re-layouts  2.45 us (3%)
    all_to_all x3, waiting for transfers between devices, spread_out(): return lax.all_to_all(value, axes, 0, 0, tiled=True)  31.2 us
    all_to_all x3, starting transfers between devices, spread_out(): return lax.all_to_all(value, axes, 0, 0, tiled=True)  22.3 us
    pallas_call x5, Pallas kernels, run_kernel(): pl.pallas_call(kernel, out_shape=outs, in_specs=[ANY] * count + [VMEM] *...  13.7 us
    ppermute x2, starting transfers between devices, relay(): return lax.ppermute(value, 'pipe', [(i, i - 1) for i in range(1, size)])  2.72 us
    unnamed x8, local copies, waits for them, and re-layouts  2.45 us
    pallas_call x1, Pallas kernels, layer(): pl.pallas_call(outer_kernel, out_shape=(shape((everyone, 1, 128), F32), s...  2.35 us
    pallas_call x1, Pallas kernels, layer(): pl.pallas_call(received_kernel, out_shape=(shape((1, 1, BLOCK, WIDTH), BF...  2.29 us
  transfers between devices with their start and end apart: 5, of which 3 were waited for; matrix products, arithmetic and copies ran while one was open for 0% of the time, Pallas kernels for 15%

commit v1 on v0

--- a/solution.py
+++ b/solution.py
@@ -85,7 +85,7 @@
     return 4 if dims[0] * dims[1] >= BLOCK * WIDTH else 1
 
 
-def run_kernel(body, fetched, held, outs, scratch=()):
+def run_kernel(body, fetched, held, outs, scratch=(), grant=24, far_outs=0):
     count, near, far = len(fetched), len(held), len(outs)
     sem_count = max(count, 1)
 
@@ -121,12 +121,12 @@
         kernel,
         out_shape=outs,
         in_specs=[ANY] * count + [VMEM] * near,
-        out_specs=tuple([VMEM] * far),
+        out_specs=tuple([ANY] * far_outs + [VMEM] * (far - far_outs)),
         scratch_shapes=[pltpu.VMEM(v.shape, v.dtype) for v in fetched]
         + [pltpu.SemaphoreType.DMA((sem_count, 4))]
         + list(scratch),
         interpret=INTERPRET,
-        compiler_params=pltpu.CompilerParams(vmem_limit_bytes=24 * 1024 * 1024),
+        compiler_params=pltpu.CompilerParams(vmem_limit_bytes=grant * 1024 * 1024),
     )(*(pltpu.with_memory_space_constraint(v, pltpu.HBM) for v in fetched), *held)
 
 
@@ -140,7 +140,12 @@
     return mm(identity(BLOCK).astype(BF16), raw_ref[...], ((1,), (1,)))
 
 
-def ends_kernel(fetch, pay_ref, time_ref):
+def ends_kernel(fetch, pay_out, time_ref, pay_ref, out_sems):
+    halves = (slice(64, 136), slice(0, 64))
+    copies = [
+        pltpu.make_async_copy(pay_ref.at[:, rows, :], pay_out.at[:, rows, :], out_sems.at[k])
+        for k, rows in enumerate(halves)
+    ]
     spread = head_of_lane().astype(BF16)
     raw = upright(fetch(0)) + fetch(2)[...]
     step = jnp.maximum(raw, 0.0) + jnp.log1p(jnp.exp(-jnp.abs(raw)))
@@ -156,15 +161,19 @@
         piece = high.astype(BF16).astype(F32)
         pay_ref[h, 128:136, :] = jnp.where(upper_half, piece, high - piece).astype(BF16)
     head = expand(jnp.exp(run), spread)
-    tail = expand(jnp.exp(last - run) * step, spread)
     gs = (fetch(3)[...].astype(F32) * head).astype(BF16)
     seen = mm(fetch(4)[...], gs, ((0,), (0,))).T.astype(BF16)
     for h in range(HEADS):
         pay_ref[h, 64:128, :] = seen[h * HEAD_DIM : (h + 1) * HEAD_DIM, :]
+    copies[0].start()
+    tail = expand(jnp.exp(last - run) * step, spread)
     xs = (fetch(5)[...].astype(F32) * tail).astype(BF16)
     end = mm(fetch(6)[...], xs, ((0,), (0,))).T.astype(BF16)
     for h in range(HEADS):
         pay_ref[h, 0:64, :] = end[h * HEAD_DIM : (h + 1) * HEAD_DIM, :]
+    copies[1].start()
+    for copy in copies:
+        copy.wait()
 
 
 PACK = WIDTH + 2 * STATE
@@ -390,6 +399,8 @@
         (raw, log_row, bias_row, g, c, x, b),
         (),
         (shape((HEADS, 136, STATE), BF16), shape((2 * BLOCK, HEADS), F32)),
+        (pltpu.VMEM((HEADS, 136, STATE), BF16), pltpu.SemaphoreType.DMA((2,))),
+        far_outs=1,
     )
     got = spread_out(pay, CTX)
     lead, pack, acc, base, blank = run_kernel(
@@ -406,7 +417,9 @@
         (pltpu.VMEM((BLOCK, WIDTH), F32), pltpu.VMEM((BLOCK, BLOCK), F32)),
     )
     lead = relay(lead)
-    (states,) = run_kernel(join_kernel, (), (got, acc), (shape((RANKS, 128, STATE), BF16),))
+    (states,) = run_kernel(
+        join_kernel, (), (got, acc), (shape((RANKS, 128, STATE), BF16),)
+    )
     states = spread_out(states, CTX)
     blank = pltpu.with_memory_space_constraint(blank, pltpu.HBM)
     par, sent = pl.pallas_call(
@@ -426,7 +439,11 @@
     sent = relay(sent)
     par = spread_out(par, DP_CTX)
     (y,) = run_kernel(
-        output_kernel, (), (states, pack, acc, base), (shape((1, 1, BLOCK, WIDTH), BF16),)
+        output_kernel,
+        (),
+        (states, pack, acc, base),
+        (shape((1, 1, BLOCK, WIDTH), BF16),),
+        grant=12,
     )
     dx, db, dc, draw = pl.pallas_call(
         received_kernel,
@@ -440,9 +457,11 @@
         out_specs=(ANY, ANY, ANY, ANY),
         scratch_shapes=[pltpu.VMEM((BLOCK, WIDTH), BF16), pltpu.SemaphoreType.DMA((14,))],
         interpret=INTERPRET,
-        compiler_params=pltpu.CompilerParams(vmem_limit_bytes=12 * 1024 * 1024),
+        compiler_params=pltpu.CompilerParams(vmem_limit_bytes=6 * 1024 * 1024),
     )(lead, sent)
-    (par,) = run_kernel(fold_kernel, (), (par,), (shape((3, 1, HEADS), F32),))
+    (par,) = run_kernel(
+        fold_kernel, (), (par,), (shape((3, 1, HEADS), F32),), grant=2
+    )
     return y, dx, db, dc, jnp.swapaxes(draw, 2, 3), jnp.swapaxes(par, 0, 1)
 
 

time: 78.4 us -> 78.2 us (level)
  no operation moved by 1% of the time
where the time goes in v1:
time: 78.2 us; the launch traced here: 77.7 us
  waiting for transfers between devices  31.3 us (40%)
  starting transfers between devices  25.1 us (32%)
  Pallas kernels  18.2 us (23%)
  local copies, waits for them, and re-layouts  2.45 us (3%)
    all_to_all x3, waiting for transfers between devices, spread_out(): return lax.all_to_all(value, axes, 0, 0, tiled=True)  31.3 us
    all_to_all x3, starting transfers between devices, spread_out(): return lax.all_to_all(value, axes, 0, 0, tiled=True)  22.3 us
    pallas_call x5, Pallas kernels, run_kernel(): pl.pallas_call(kernel, out_shape=outs, in_specs=[ANY] * count + [VMEM] *...  13.5 us
    ppermute x2, starting transfers between devices, relay(): return lax.ppermute(value, 'pipe', [(i, i - 1) for i in range(1, size)])  2.72 us
    unnamed x8, local copies, waits for them, and re-layouts  2.45 us
    pallas_call x1, Pallas kernels, layer(): pl.pallas_call(outer_kernel, out_shape=(shape((everyone, 1, 128), F32), s...  2.35 us
    pallas_call x1, Pallas kernels, layer(): pl.pallas_call(received_kernel, out_shape=(shape((1, 1, BLOCK, WIDTH), BF...  2.29 us
  transfers between devices with their start and end apart: 5, of which 3 were waited for; matrix products, arithmetic and copies ran while one was open for 0% of the time, Pallas kernels for 15%

profile of v1, /device:TPU:1, one launch (start us, length us, event | category | flops | bytes accessed | tf_op | source)
XLA Modules:
  0.0 77.7 jit_solution(3723657646583361794)
XLA Ops:
  0.6 3.5 %shard_map.127 = (bf16[16,136,128]{2,1,0:T(8,128)(2,1)}, f32[512,16]{1,0:T(8,128)S(1)}) custom-call(bf16[16,256]{1,0:T(8,128)(2,1)} %bitcast.17, f32[1,16]{1,0:T(1,128)} %refs_5_.1, f32[1,16]{1,0:T(1,128)} %refs_6_.1, bf16[256,1024]{1,0:T(8,128)(2,1)} %bitcast.9, bf16[256,128]{1,0:T(8,128)(2,1)} %bitcast.13, bf16[256,1024]{1,0:T(8,128)(2,1)} %bitcast.11, ...), custom_call_target="tpu_custom_call" | custom-call | tf_op jit(solution)/shard_map/pallas_call | solution.py:120
  4.2 13.9 %all-to-all-start = ((bf16[16,136,128]{2,1,0:T(8,128)(2,1)}), bf16[16,136,128]{2,1,0:T(8,128)(2,1)S(1)}, u32[]{:S(2)}, u32[]{:S(2)}) async-start(bf16[16,136,128]{2,1,0:T(8,128)(2,1)} %get-tuple-element.19), calls=%async_computation | async-start | bytes 1114112 | tf_op jit(solution)/shard_map/all_to_all | solution.py:383
  18.0 6.3 %shard_map.128 = (bf16[256,1280]{1,0:T(8,128)(2,1)S(1)}, bf16[256,2304]{1,0:T(8,128)(2,1)S(1)}, f32[256,384]{1,0:T(8,128)S(1)}, f32[256,1024]{1,0:T(8,128)S(1)}, f32[64,1,128]{2,1,0:T(1,128)S(1)}) custom-call(bf16[256,1024]{1,0:T(8,128)(2,1)} %bitcast.12, bf16[256,1024]{1,0:T(8,128)(2,1)} %bitcast.10, bf16[256,128]{1,0:T(8,128)(2,1)} %bitcast.16, ...), custom_call_target="tpu_custom_call" | custom-call | tf_op jit(solution)/shard_map/pallas_call | solution.py:120
  24.3 0.0 copy-start
  24.3 1.0 %copy-done = f32[256,1024]{1,0:T(8,128)} copy-done((f32[256,1024]{1,0:T(8,128)}, f32[256,1024]{1,0:T(8,128)S(1)}, u32[]{:S(2)}) %copy-start) | copy-done | bytes 1048600
  25.3 0.0 copy-start.2
  25.3 0.6 copy-done.2
  25.9 0.9 %copy-done.3 = bf16[256,1280]{1,0:T(8,128)(2,1)} copy-done((bf16[256,1280]{1,0:T(8,128)(2,1)}, bf16[256,1280]{1,0:T(8,128)(2,1)S(1)}, u32[]{:S(2)}) %copy-start.3) | copy-done | bytes 655384
  26.8 9.2 %all-to-all-done.refs_0_ = bf16[16,136,128]{2,1,0:T(8,128)(2,1)S(1)} async-done(((bf16[16,136,128]{2,1,0:T(8,128)(2,1)}), bf16[16,136,128]{2,1,0:T(8,128)(2,1)S(1)}, u32[]{:S(2)}, u32[]{:S(2)}) %all-to-all-start) | async-done | bytes 557088 | tf_op jit(solution)/shard_map/all_to_all | solution.py:383
  36.0 1.0 %shard_map.129 = bf16[16,128,128]{2,1,0:T(8,128)(2,1)} custom-call(bf16[16,136,128]{2,1,0:T(8,128)(2,1)S(1)} %all-to-all-done.refs_0_, f32[256,384]{1,0:T(8,128)S(1)} %get-tuple-element.21.refs_1_.refs_2_.acc_ref), custom_call_target="tpu_custom_call" | custom-call | tf_op jit(solution)/shard_map/pallas_call | solution.py:120
  37.0 3.5 %all-to-all-start.1 = ((bf16[16,128,128]{2,1,0:T(8,128)(2,1)}), bf16[16,128,128]{2,1,0:T(8,128)(2,1)S(1)}, u32[]{:S(2)}, u32[]{:S(2)}) async-start(bf16[16,128,128]{2,1,0:T(8,128)(2,1)} %shard_map.129), calls=%async_computation.1 | async-start | bytes 1048576 | tf_op jit(solution)/shard_map/all_to_all | solution.py:383
  40.5 0.0 copy-start.1
  40.5 1.4 %collective-permute-start = (bf16[256,1280]{1,0:T(8,128)(2,1)}, bf16[256,1280]{1,0:T(8,128)(2,1)}, u32[]{:S(2)}, u32[]{:S(2)}) collective-permute-start(bf16[256,1280]{1,0:T(8,128)(2,1)} %copy-done.3), channel_id=1, source_target_pairs={{16,0},{32,16},{48,32},{64,48},{80,64},{96,80},{112,96},{128,112},... | collective-permute-start | bytes 1966088 | tf_op jit(solution)/shard_map/ppermute | solution.py:388
  41.9 15.2 %all-to-all-done.1.refs_0_.state_ref = bf16[16,128,128]{2,1,0:T(8,128)(2,1)S(1)} async-done(((bf16[16,128,128]{2,1,0:T(8,128)(2,1)}), bf16[16,128,128]{2,1,0:T(8,128)(2,1)S(1)}, u32[]{:S(2)}, u32[]{:S(2)}) %all-to-all-start.1) | async-done | bytes 524320 | tf_op jit(solution)/shard_map/all_to_all | solution.py:383
  57.1 2.3 %shard_map.131 = (f32[64,1,128]{2,1,0:T(1,128)}, bf16[25,64,128]{2,1,0:T(8,128)(2,1)}) custom-call(f32[64,1,128]{2,1,0:T(1,128)} %copy-done.2, bf16[16,128,128]{2,1,0:T(8,128)(2,1)S(1)} %all-to-all-done.1.refs_0_.state_ref, bf16[256,2304]{1,0:T(8,128)(2,1)S(1)} %get-tuple-element.22.refs_1_.pack_ref, ...), custom_call_target="tpu_custom_call", output_to_operand_aliasing={{0}: (0, {})} | custom-call | tf_op jit(solution)/shard_map/pallas_call | solution.py:425
  59.5 1.3 %collective-permute-start.1 = (bf16[25,64,128]{2,1,0:T(8,128)(2,1)}, bf16[25,64,128]{2,1,0:T(8,128)(2,1)S(1)}, u32[]{:S(2)}, u32[]{:S(2)}) collective-permute-start(bf16[25,64,128]{2,1,0:T(8,128)(2,1)} %get-tuple-element.26), channel_id=1, source_target_pairs={{16,0},{32,16},{48,32},{64,48},{80,64},{96,80},{112,96},{128,112},... | collective-permute-start | bytes 1228808 | tf_op jit(solution)/shard_map/ppermute | solution.py:388
  60.8 5.0 %all-to-all-start.2 = ((f32[64,1,128]{2,1,0:T(1,128)}), f32[64,1,128]{2,1,0:T(1,128)}, u32[]{:S(2)}, u32[]{:S(2)}) async-start(f32[64,1,128]{2,1,0:T(1,128)} %get-tuple-element.31), calls=%async_computation.2 | async-start | bytes 65536 | tf_op jit(solution)/shard_map/all_to_all | solution.py:383
  65.8 0.0 copy-done.1
  65.8 1.3 %shard_map.130 = bf16[1,1,256,1024]{3,2,1,0:T(8,128)(2,1)} custom-call(bf16[16,128,128]{2,1,0:T(8,128)(2,1)S(1)} %all-to-all-done.1.refs_0_.state_ref, bf16[256,2304]{1,0:T(8,128)(2,1)S(1)} %get-tuple-element.22.refs_1_.pack_ref, f32[256,384]{1,0:T(8,128)S(1)} %get-tuple-element.21.refs_1_.refs_2_.acc_ref, f32[256,1024]{1,0:T(8,128)S(1)} %copy-done.1), custom_call_target="tpu_custom_call" | custom-call | tf_op jit(solution)/shard_map/pallas_call | solution.py:120
  67.1 6.8 %all-to-all-done.2.refs_0_ = f32[64,1,128]{2,1,0:T(1,128)} async-done(((f32[64,1,128]{2,1,0:T(1,128)}), f32[64,1,128]{2,1,0:T(1,128)}, u32[]{:S(2)}, u32[]{:S(2)}) %all-to-all-start.2) | async-done | bytes 32800 | tf_op jit(solution)/shard_map/all_to_all | solution.py:383
  73.9 1.5 %shard_map.133 = f32[3,1,16]{2,1,0:T(1,128)} custom-call(f32[64,1,128]{2,1,0:T(1,128)} %all-to-all-done.2.refs_0_), custom_call_target="tpu_custom_call" | custom-call | tf_op jit(solution)/shard_map/pallas_call | solution.py:120
  75.4 0.0 collective-permute-done.lead_ref
  75.4 0.0 collective-permute-done.1.sent_ref
  75.4 2.3 %shard_map.132 = (bf16[1,1,256,1024]{3,2,1,0:T(8,128)(2,1)}, bf16[1,1,256,128]{3,2,1,0:T(8,128)(2,1)}, bf16[1,1,256,128]{3,2,1,0:T(8,128)(2,1)}, bf16[1,1,16,256]{3,2,1,0:T(8,128)(2,1)}) custom-call(bf16[256,1280]{1,0:T(8,128)(2,1)} %collective-permute-done.lead_ref, bf16[25,64,128]{2,1,0:T(8,128)(2,1)S(1)} %collective-permute-done.1.sent_ref), custom_call_target="tpu_custom_call" | custom-call | tf_op jit(solution)/shard_map/pallas_call | solution.py:448
  (1 shorter events, 0.0 us)
Async XLA Ops:
  4.2 31.8 %all-to-all-start = ((bf16[16,136,128]{2,1,0:T(8,128)(2,1)}), bf16[16,136,128]{2,1,0:T(8,128)(2,1)S(1)}, u32[]{:S(2)}, u32[]{:S(2)}) async-start(bf16[16,136,128]{2,1,0:T(8,128)(2,1)} %get-tuple-element.19), calls=%async_computation | async-start | bytes 1114112 | tf_op jit(solution)/shard_map/all_to_all | solution.py:383
  24.3 1.0 %copy-start = (f32[256,1024]{1,0:T(8,128)}, f32[256,1024]{1,0:T(8,128)S(1)}, u32[]{:S(2)}) copy-start(f32[256,1024]{1,0:T(8,128)S(1)} %get-tuple-element.23.refs_3_) | copy-start | bytes 3145732
  25.3 0.6 copy-start.2
  25.9 0.9 %copy-start.3 = (bf16[256,1280]{1,0:T(8,128)(2,1)}, bf16[256,1280]{1,0:T(8,128)(2,1)S(1)}, u32[]{:S(2)}) copy-start(bf16[256,1280]{1,0:T(8,128)(2,1)S(1)} %get-tuple-element.24) | copy-start | bytes 1966084
  37.0 20.1 %all-to-all-start.1 = ((bf16[16,128,128]{2,1,0:T(8,128)(2,1)}), bf16[16,128,128]{2,1,0:T(8,128)(2,1)S(1)}, u32[]{:S(2)}, u32[]{:S(2)}) async-start(bf16[16,128,128]{2,1,0:T(8,128)(2,1)} %shard_map.129), calls=%async_computation.1 | async-start | bytes 1048576 | tf_op jit(solution)/shard_map/all_to_all | solution.py:383
  40.5 25.3 %copy-start.1 = (f32[256,1024]{1,0:T(8,128)S(1)}, f32[256,1024]{1,0:T(8,128)}, u32[]{:S(2)}) copy-start(f32[256,1024]{1,0:T(8,128)} %copy-done) | copy-start | bytes 3145732
  40.5 34.9 %collective-permute-start = (bf16[256,1280]{1,0:T(8,128)(2,1)}, bf16[256,1280]{1,0:T(8,128)(2,1)}, u32[]{:S(2)}, u32[]{:S(2)}) collective-permute-start(bf16[256,1280]{1,0:T(8,128)(2,1)} %copy-done.3), channel_id=1, source_target_pairs={{16,0},{32,16},{48,32},{64,48},{80,64},{96,80},{112,96},{128,112},... | collective-permute-start | bytes 1966088 | tf_op jit(solution)/shard_map/ppermute | solution.py:388
  59.5 15.9 %collective-permute-start.1 = (bf16[25,64,128]{2,1,0:T(8,128)(2,1)}, bf16[25,64,128]{2,1,0:T(8,128)(2,1)S(1)}, u32[]{:S(2)}, u32[]{:S(2)}) collective-permute-start(bf16[25,64,128]{2,1,0:T(8,128)(2,1)} %get-tuple-element.26), channel_id=1, source_target_pairs={{16,0},{32,16},{48,32},{64,48},{80,64},{96,80},{112,96},{128,112},... | collective-permute-start | bytes 1228808 | tf_op jit(solution)/shard_map/ppermute | solution.py:388
  60.8 13.1 %all-to-all-start.2 = ((f32[64,1,128]{2,1,0:T(1,128)}), f32[64,1,128]{2,1,0:T(1,128)}, u32[]{:S(2)}, u32[]{:S(2)}) async-start(f32[64,1,128]{2,1,0:T(1,128)} %get-tuple-element.31), calls=%async_computation.2 | async-start | bytes 65536 | tf_op jit(solution)/shard_map/all_to_all | solution.py:383
